TPU v7x, 256 devices: a whole 4x4x8 slice. The times are simulated.
256 devices in a mesh: band: 8 (over z), dev: 32 (over x, y, core).
Axes of the slice: x: 4, y: 4, z: 8, core: 2. Of those that a mesh axis runs over, the one named last changes fastest.
Arguments:
- anomaly: float32 [256, 1048576], P('dev', 'band'), may hold values from -6 to 6
- ocean_mask: int32 [1048576], P('band'), may hold values 0 or 1
- area_weight: float32 [1048576], P('band'), may hold values from 0.02 to 1
Outputs:
- factor: float32 [256, 256], replicated
- scores: float32 [256, 1048576], P(None, ('band', 'dev'))
All inputs are finite; a program needn't handle non-finite values. No bound on the sum of `ocean_mask` on one device may be relied on, other than what follows from the above.
Results may differ from a plain program's by a relative error of at most 0.000075.
Values sent between devices are 32-bit elements; how exact they have to be, the bound alone decides.
A program may use at most 64 MiB of HBM per device.

v0:
```python
import jax
import jax.numpy as jnp
from jax import lax
from jax.sharding import PartitionSpec as P


def on_device(anomaly, ocean_mask, area_weight):
    weights = area_weight * ocean_mask.astype(jnp.float32)
    local_scaled = anomaly * jnp.sqrt(weights)[None, :]
    group_size = lax.axis_size("dev")
    own_cells = weights.shape[0] // group_size
    own_weights = lax.dynamic_slice_in_dim(weights, lax.axis_index("dev") * own_cells, own_cells, 0)
    partial_total = jnp.sum(own_weights)
    scaled = lax.all_to_all(local_scaled, "dev", split_axis=1, concat_axis=0, tiled=True)
    partial_gram = jnp.dot(scaled, scaled.T, precision=lax.Precision.HIGHEST)
    gram, total = lax.psum((partial_gram, partial_total), ("band", "dev"))
    lower = jnp.linalg.cholesky(gram / total)
    scores = lax.linalg.triangular_solve(lower, scaled, left_side=True, lower=True)
    return (lower.T, scores)


def solution(mesh):
    return jax.shard_map(
        on_device,
        mesh=mesh,
        in_specs=(P("dev", "band"), P("band"), P("band")),
        out_specs=(P(), P(None, ("band", "dev"))),
        check_vma=False,
    )
```

profile of v0, /device:TPU:1, one launch (start us, length us, event | category | flops | bytes accessed | tf_op | source)
XLA Modules:
  0.0 409.8 jit_solution(14869644310885381661)
XLA Ops:
  7.2 0.0 all-reduce.3.cloned.1.call-start
  7.2 1.4 fusion.11
  8.6 2.7 broadcast_multiply_fusion
  11.3 59.0 %all_to_all.19 = f32[8,32,4096]{2,0,1:T(8,128)S(1)} all-to-all(f32[8,32,4096]{2,0,1:T(8,128)S(1)} %bitcast.48), channel_id=1, replica_groups=mesh['band'=8,'dev'=32] {'dev'}, dimensions={1} | all-to-all | bytes 8388608 | tf_op jit(solution)/shard_map/all_to_all | solution.py:14
  70.3 2.0 copy-done
  72.3 4.2 %fusion = f32[256,256]{0,1:T(8,128)} fusion(f32[8,32,4096]{2,0,1:T(8,128)S(1)} %all_to_all.19), kind=kOutput, calls=%fused_computation.4 | convolution fusion | flops 3221225472 | bytes 4456448 | tf_op jit(solution)/shard_map/dot_general | solution.py:15
  76.5 0.0 all-reduce.3.cloned.1.call-update
  76.6 0.6 dynamic-slice_reduce_fusion
  77.2 78.2 %psum.15 = f32[]{:T(128)} all-reduce(f32[]{:T(128)} %dynamic-slice_reduce_fusion), channel_id=1, replica_groups=mesh['band'=8,'dev'=32] {'band','dev'}, use_global_device_ids=true, to_apply=%region_2.0 | all-reduce | flops 1 | bytes 8 | tf_op jit(solution)/shard_map/psum | solution.py:16
  155.4 173.4 %all-reduce.3.cloned.1.call-done = f32[256,256]{0,1:T(8,128)} async-done(((f32[256,256]{0,1:T(8,128)}), f32[256,256]{0,1:T(8,128)}) %all-reduce.3.cloned.1.call-update) | async-done | bytes 262160 | tf_op jit(solution)/shard_map/psum | solution.py:16
  328.7 1.6 broadcast_divide_fusion
  330.3 0.1 copy.6
  330.5 1.6 fusion.3
  332.1 11.7 %cholesky.50 = f32[128,128]{1,0:T(8,128)S(1)} custom-call(f32[128,128]{1,0:T(8,128)S(1)} %cholesky.118), custom_call_target="Cholesky" | custom-call | tf_op jit(solution)/shard_map/jit(cholesky)/cholesky | solution.py:17
  343.9 9.8 %custom-call.14 = f32[1,128,128]{1,2,0:T(8,128)S(1)} custom-call(f32[1,128,128]{2,1,0:T(8,128)S(1)} %get-tuple-element.29), custom_call_target="InvertDiagBlocksLowerTriangular" | custom-call | tf_op jit(solution)/shard_map/jit(cholesky)/cholesky | solution.py:17
  353.7 0.2 constant_dynamic-update-slice_fusion.1
  353.9 0.3 convolution_subtract_fusion.1
  354.2 11.7 %cholesky.105 = f32[128,128]{1,0:T(8,128)S(1)} custom-call(f32[128,128]{1,0:T(8,128)S(1)} %convolution_subtract_fusion.1), custom_call_target="Cholesky" | custom-call | tf_op jit(solution)/shard_map/jit(cholesky)/cholesky | solution.py:17
  365.9 0.7 compare_reduce_fusion
  368.1 0.8 copy.7
  368.9 0.1 triangular_solve.46
  369.0 4.1 while.1
  369.0 0.7 fusion.18
  369.6 1.3 bitcast_dynamic-update-slice_fusion.2
  371.0 0.7 fusion.18
  371.7 1.3 bitcast_dynamic-update-slice_fusion.2
  373.0 19.9 %custom-call.15 = f32[2,128,128]{1,2,0:T(8,128)S(1)} custom-call(f32[2,128,128]{2,1,0:T(8,128)S(1)} %get-tuple-element.9), custom_call_target="InvertDiagBlocksLowerTriangular" | custom-call | tf_op jit(solution)/shard_map/triangular_solve | solution.py:18
  392.9 0.0 copy-start.1
  392.9 3.7 fusion.2
  396.6 1.9 convolution_subtract_fusion
  398.5 1.9 fusion.7
  400.5 2.5 pad_maximum_fusion
  (11 shorter events, 0.2 us)
Async XLA Ops:
  7.2 321.6 %all-reduce.3.cloned.1.call-start = ((), (), s32[]{:S(2)}) async-start(), calls=%async_computation.1 | async-start | bytes 524288 | tf_op jit(solution)/shard_map/psum | solution.py:16
  70.3 2.0 copy-start
  392.9 3.7 copy-start.1
Sparse Core Ops, SparseCore 0:
  76.7 252.0 all-reduce.2
where the time goes:
time: 411 us; the launch traced here: 410 us
  waiting for transfers between devices  173 us (42%)
  blocking collectives  137 us (33%)
  other arithmetic  64.4 us (16%)
  between operations  15.5 us (4%)
  matrix products  12.2 us (3%)
  local copies, waits for them, and re-layouts  7.1 us (2%)
    psum x1, waiting for transfers between devices, on_device(): gram, total = lax.psum((partial_gram, partial_total), ('band', 'dev'))  173 us
    psum x1, blocking collectives, on_device(): gram, total = lax.psum((partial_gram, partial_total), ('band', 'dev'))  78.2 us
    all_to_all x1, blocking collectives, on_device(): lax.all_to_all(local_scaled, 'dev', split_axis=1, concat_axis=0, tiled=True)  59 us
    another operation x6, other arithmetic, on_device(): lower = jnp.linalg.cholesky(gram / total)  34 us
    another operation x4, other arithmetic, on_device(): lax.linalg.triangular_solve(lower, scaled, left_side=True, lower=True)  22.4 us
  transfers between devices with their start and end apart: 1, of which 1 were waited for; matrix products, arithmetic and copies ran while one was open for 0% of the time, Pallas kernels for 0%

commit v1 on v0

v1 whole, which is shorter than its diff:
```python
import functools
import jax
import jax.numpy as jnp
from jax import lax
from jax.experimental import pallas as pl
from jax.experimental.pallas import tpu as pltpu
from jax.sharding import PartitionSpec as P

MESH = pl.DeviceIdType.MESH
CHUNKS = 4


def gather_gram(n_band, n_dev, anomaly, area, mask, own_area, own_mask, hi_out, lo_out, gram_out,
                land, hi, lo, hh, hl, part, piece_in, zsend, zin, agsend, gsum,
                load_sem, a2a_send, a2a_recv, rs_send, rs_recv, z_send, z_recv, ag_send, ag_recv, out_sem):
    z = lax.axis_index("band")
    me = lax.axis_index("dev")
    snaps, cells = land.shape
    rows = snaps // n_dev
    width = cells // CHUNKS

    barrier = pltpu.get_barrier_semaphore()

    def greet(i, _):
        pl.semaphore_signal(barrier, inc=1, device_id=(z, lax.rem(me + i, n_dev)), device_id_type=MESH)
        return _

    def greet_z(i, _):
        pl.semaphore_signal(barrier, inc=1, device_id=(lax.rem(z + i, n_band), me), device_id_type=MESH)
        return _

    lax.fori_loop(1, n_dev, greet, 0)
    lax.fori_loop(1, n_band, greet_z, 0)
    own = pltpu.make_async_copy(anomaly.at[:, pl.ds(pl.multiple_of(me * cells, cells), cells)],
                                land.at[pl.ds(pl.multiple_of(me * rows, rows), rows), :], load_sem)
    own.start()
    pl.semaphore_wait(barrier, n_dev - 1 + n_band - 1)

    for c in range(CHUNKS):
        def send(i, _, c=c):
            to = lax.rem(me + i, n_dev)
            pltpu.make_async_remote_copy(
                src_ref=anomaly.at[:, pl.ds(pl.multiple_of(to * cells + c * width, width), width)],
                dst_ref=land.at[pl.ds(pl.multiple_of(me * rows, rows), rows), pl.ds(c * width, width)],
                send_sem=a2a_send.at[c], recv_sem=a2a_recv.at[c],
                device_id=(z, to), device_id_type=MESH).start()
            return _
        lax.fori_loop(1, n_dev, send, 0)

    band_total = jnp.sum(area[...] * mask[...].astype(jnp.float32))
    root = jnp.sqrt(own_area[...] * own_mask[...].astype(jnp.float32))
    hh[...] = jnp.zeros_like(hh)
    hl[...] = jnp.zeros_like(hl)
    own.wait()
    nt = (((1,), (1,)), ((), ()))
    for c in range(CHUNKS):
        window = land.at[pl.ds(0, rows * (n_dev - 1)), pl.ds(c * width, width)]
        pltpu.make_async_copy(window, window, a2a_recv.at[c]).wait()
        for t in range(width // 128):
            k = c * (width // 128) + t
            at = pl.ds(k * 128, 128)
            x = land[:, at] * root[k:k + 1, :]
            top = x.astype(jnp.bfloat16)
            hi[:, at] = top
            lo[:, at] = (x - top.astype(jnp.float32)).astype(jnp.bfloat16)
        at = pl.ds(c * width, width)
        hh[...] += lax.dot_general(hi[:, at], hi[:, at], nt, preferred_element_type=jnp.float32)
        hl[...] += lax.dot_general(hi[:, at], lo[:, at], nt, preferred_element_type=jnp.float32)
    put_hi = pltpu.make_async_copy(hi, hi_out, out_sem.at[0])
    put_lo = pltpu.make_async_copy(lo, lo_out, out_sem.at[1])
    put_hi.start()
    put_lo.start()
    part[...] = (hh[...] + (hl[...] + hl[...].T)).reshape(n_dev, rows, snaps)

    def send_piece(i, _):
        to = lax.rem(me + i, n_dev)
        pltpu.make_async_remote_copy(
            src_ref=part.at[to], dst_ref=piece_in.at[me], send_sem=rs_send, recv_sem=rs_recv,
            device_id=(z, to), device_id_type=MESH).start()
        return _
    lax.fori_loop(1, n_dev, send_piece, 0)
    piece_in[me] = part[me]
    some = piece_in.at[pl.ds(0, n_dev - 1)]
    pltpu.make_async_copy(some, some, rs_recv).wait()
    piece = jnp.sum(piece_in[...], axis=0)

    zsend[:, :snaps] = piece
    zsend[:, snaps:] = jnp.full((rows, 128), band_total, jnp.float32)
    zin[z] = zsend[...]

    def send_z(i, _):
        pltpu.make_async_remote_copy(
            src_ref=zsend, dst_ref=zin.at[z], send_sem=z_send, recv_sem=z_recv,
            device_id=(lax.rem(z + i, n_band), me), device_id_type=MESH).start()
        return _
    lax.fori_loop(1, n_band, send_z, 0)
    some_z = zin.at[pl.ds(0, n_band - 1)]
    pltpu.make_async_copy(some_z, some_z, z_recv).wait()
    summed = jnp.sum(zin[...], axis=0)
    total = summed[:, snaps:]
    agsend[...] = summed[:, :snaps] / jnp.concatenate([total, total], axis=1)
    gsum[me] = agsend[...]

    def send_sum(i, _):
        pltpu.make_async_remote_copy(
            src_ref=agsend, dst_ref=gsum.at[me], send_sem=ag_send, recv_sem=ag_recv,
            device_id=(z, lax.rem(me + i, n_dev)), device_id_type=MESH).start()
        return _
    lax.fori_loop(1, n_dev, send_sum, 0)
    some_g = gsum.at[pl.ds(0, n_dev - 1)]
    pltpu.make_async_copy(some_g, some_g, ag_recv).wait()
    gram_out[...] = gsum[...].reshape(snaps, snaps)
    pltpu.make_async_copy(some, some, rs_send).wait()
    pltpu.make_async_copy(some_z, some_z, z_send).wait()
    pltpu.make_async_copy(some_g, some_g, ag_send).wait()
    for c in range(CHUNKS):
        window = land.at[pl.ds(0, rows * (n_dev - 1)), pl.ds(c * width, width)]
        pltpu.make_async_copy(window, window, a2a_send.at[c]).wait()
    put_hi.wait()
    put_lo.wait()


def call_gather_gram(mesh, anomaly, ocean_mask, area_weight):
    n_band, n_dev = mesh.shape["band"], mesh.shape["dev"]
    rows, band_cells = anomaly.shape
    snaps, cells = rows * n_dev, band_cells // n_dev
    area2 = area_weight.reshape(band_cells // 128, 128)
    mask2 = ocean_mask.reshape(band_cells // 128, 128)
    at = lax.axis_index("dev") * (cells // 128)
    own_area = lax.dynamic_slice_in_dim(area2, at, cells // 128, 0)
    own_mask = lax.dynamic_slice_in_dim(mask2, at, cells // 128, 0)
    f32, bf16 = jnp.float32, jnp.bfloat16
    vmem = pl.BlockSpec(memory_space=pltpu.VMEM)
    hbm = pl.BlockSpec(memory_space=pl.ANY)
    dma = pltpu.SemaphoreType.DMA
    return pl.pallas_call(
        functools.partial(gather_gram, n_band, n_dev),
        name="gather_gram",
        out_shape=(jax.ShapeDtypeStruct((snaps, cells), bf16), jax.ShapeDtypeStruct((snaps, cells), bf16),
                   jax.ShapeDtypeStruct((snaps, snaps), f32)),
        in_specs=[hbm, vmem, vmem, vmem, vmem],
        out_specs=(hbm, hbm, vmem),
        scratch_shapes=[
            pltpu.VMEM((snaps, cells), f32), pltpu.VMEM((snaps, cells), bf16), pltpu.VMEM((snaps, cells), bf16),
            pltpu.VMEM((snaps, snaps), f32), pltpu.VMEM((snaps, snaps), f32),
            pltpu.VMEM((n_dev, rows, snaps), f32), pltpu.VMEM((n_dev, rows, snaps), f32),
            pltpu.VMEM((rows, snaps + 128), f32), pltpu.VMEM((n_band, rows, snaps + 128), f32),
            pltpu.VMEM((rows, snaps), f32), pltpu.VMEM((n_dev, rows, snaps), f32),
            dma, dma((CHUNKS,)), dma((CHUNKS,)), dma, dma, dma, dma, dma, dma, dma((2,)),
        ],
        compiler_params=pltpu.CompilerParams(collective_id=0, has_side_effects=True, vmem_limit_bytes=40 * 1024 * 1024),
        cost_estimate=pl.CostEstimate(flops=4 * snaps * snaps * cells, bytes_accessed=8 * snaps * cells, transcendentals=0),
    )(anomaly, area2, mask2, own_area, own_mask)


def solution(mesh):
    def on_device(anomaly, ocean_mask, area_weight):
        hi, lo, gram = call_gather_gram(mesh, anomaly, ocean_mask, area_weight)
        lower = jnp.linalg.cholesky(gram)
        scaled = hi.astype(jnp.float32) + lo.astype(jnp.float32)
        scores = lax.linalg.triangular_solve(lower, scaled, left_side=True, lower=True)
        return (lower.T, scores)

    return jax.shard_map(
        on_device,
        mesh=mesh,
        in_specs=(P("dev", "band"), P("band"), P("band")),
        out_specs=(P(), P(None, ("band", "dev"))),
        check_vma=False,
    )
```

time: 411 us -> 165 us (0.40)
  waiting for transfers between devices: 173 us -> 0 us
  blocking collectives: 137 us -> 0 us
  Pallas kernels: 0 us -> 84.4 us
  between operations: 15.5 us -> 2.05 us
  other arithmetic: 64.4 us -> 59.1 us
  matrix products: 12.2 us -> 7.99 us
    psum x1 -> x0, waiting for transfers between devices: 173 us -> none  [on_device(): gram, total = lax.psum((partial_gram, partial_total), ('band', 'dev'))]
    pallas_call x0 -> x1, Pallas kernels: none -> 84.4 us  [call_gather_gram(): pl.pallas_call(functools.partial(gather_gram, n_band, n_dev), name='gathe...]
    psum x1 -> x0, blocking collectives: 78.2 us -> none  [on_device(): gram, total = lax.psum((partial_gram, partial_total), ('band', 'dev'))]
    all_to_all x1 -> x0, blocking collectives: 59 us -> none  [on_device(): lax.all_to_all(local_scaled, 'dev', split_axis=1, concat_axis=0, tiled=True)]
    dot_general x1 -> x0, matrix products: 4.23 us -> none  [on_device(): partial_gram = jnp.dot(scaled, scaled.T, precision=lax.Precision.HIGHEST)]
  transfers between devices with their start and end apart: 1 -> 0, of which waited for: 1 -> 0; matrix products, arithmetic and copies ran while one was open for 0% -> 0% of each run, Pallas kernels for 0% -> 0%
where the time goes in v1:
time: 165 us; the launch traced here: 164 us
  Pallas kernels  84.4 us (51%)
  other arithmetic  59.1 us (36%)
  local copies, waits for them, and re-layouts  10.7 us (6%)
  matrix products  7.99 us (5%)
  between operations  2.05 us (1%)
    pallas_call x1, Pallas kernels, call_gather_gram(): pl.pallas_call(functools.partial(gather_gram, n_band, n_dev), name='gathe...  84.4 us
    another operation x6, other arithmetic, on_device(): lower = jnp.linalg.cholesky(gram)  34 us
    another operation x4, other arithmetic, on_device(): lax.linalg.triangular_solve(lower, scaled, left_side=True, lower=True)  22.4 us
    another operation x3, matrix products, on_device(): lax.linalg.triangular_solve(lower, scaled, left_side=True, lower=True)  7.52 us
    unnamed x9, local copies, waits for them, and re-layouts  5.11 us
    another operation x6, local copies, waits for them, and re-layouts  3.95 us

profile of v1, /device:TPU:1, one launch (start us, length us, event | category | flops | bytes accessed | tf_op | source)
XLA Modules:
  0.0 164.3 jit_solution(10852604701673635306)
XLA Ops:
  0.6 0.1 triangular_solve.42
  0.7 0.7 constant_dynamic-slice_fusion.1.own_mask
  1.4 0.7 constant_dynamic-slice_fusion.2.own_area
  2.2 0.0 copy-start
  2.2 2.2 %copy-done = f32[8,131072]{1,0:T(8,128)S(1)} copy-done((f32[8,131072]{1,0:T(8,128)S(1)}, f32[8,131072]{1,0:T(8,128)}, u32[]{:S(2)}) %copy-start) | copy-done | bytes 4194328
  4.3 0.0 copy-start.1
  4.3 1.0 copy-done.1
  5.4 0.0 copy-start.2
  5.4 1.0 copy-done.2
  6.4 84.4 %gather_gram.1 = (bf16[256,4096]{1,0:T(8,128)(2,1)S(1)}, bf16[256,4096]{1,0:T(8,128)(2,1)S(1)}, f32[256,256]{1,0:T(8,128)S(1)}) custom-call(f32[8,131072]{1,0:T(8,128)S(1)} %copy-done, f32[1024,128]{1,0:T(8,128)S(1)} %bitcast.36, s32[1024,128]{1,0:T(8,128)S(1)} %bitcast.38, f32[32,128]{1,0:T(8,128)S(1)} %constant_dynamic-slice_fusion.2.own_area, ...), custom_call_target="tpu_custom_call" | custom-call | flops 1073741824 | bytes 8388608 | tf_op jit(solution)/shard_map/gather_gram/pallas_call | solution.py:136
  90.8 2.7 %convert_add_fusion = f32[256,4096]{1,0:T(8,128)} fusion(bf16[256,4096]{1,0:T(8,128)(2,1)S(1)} %get-tuple-element.7, bf16[256,4096]{1,0:T(8,128)(2,1)S(1)} %get-tuple-element.6), kind=kLoop, calls=%fused_computation.4 | loop fusion | flops 3145728 | bytes 8388608 | tf_op jit(solution)/shard_map/add | solution.py:160
  93.6 0.1 copy.5
  93.8 11.7 %cholesky.50 = f32[128,128]{1,0:T(8,128)S(1)} custom-call(f32[128,128]{1,0:T(8,128)S(1)} %cholesky.118), custom_call_target="Cholesky" | custom-call | tf_op jit(solution)/shard_map/jit(cholesky)/cholesky | solution.py:159
  105.5 9.8 %custom-call.14 = f32[1,128,128]{1,2,0:T(8,128)S(1)} custom-call(f32[1,128,128]{2,1,0:T(8,128)S(1)} %get-tuple-element.33), custom_call_target="InvertDiagBlocksLowerTriangular" | custom-call | tf_op jit(solution)/shard_map/jit(cholesky)/cholesky | solution.py:159
  115.3 0.2 constant_dynamic-update-slice_fusion
  115.6 0.3 convolution_subtract_fusion.1
  115.8 11.7 %cholesky.105 = f32[128,128]{1,0:T(8,128)S(1)} custom-call(f32[128,128]{1,0:T(8,128)S(1)} %convolution_subtract_fusion.1), custom_call_target="Cholesky" | custom-call | tf_op jit(solution)/shard_map/jit(cholesky)/cholesky | solution.py:159
  127.6 0.7 compare_reduce_fusion
  129.6 0.8 copy.6
  130.4 4.0 %while.1 = (s32[]{:T(128)}, f32[256,256]{1,0:T(8,128)S(1)}, s32[2,2]{1,0:T(2,128)S(1)}, f32[2,128,128]{2,1,0:T(8,128)S(1)}, s32[]{:T(128)}) while((s32[]{:T(128)}, f32[256,256]{1,0:T(8,128)S(1)}, s32[2,2]{1,0:T(2,128)S(1)}, f32[2,128,128]{2,1,0:T(8,128)S(1)}, s32[]{:T(128)}) %tuple.29), condition=%wide.while_cond, body=%wide.while_body.sunk | while | flops 2 | bytes 131189 | solution.py:161
  130.4 0.6 fusion.16
  131.0 1.4 bitcast_dynamic-update-slice_fusion.2
  132.4 0.6 fusion.16
  133.0 1.4 bitcast_dynamic-update-slice_fusion.2
  134.4 19.9 %custom-call.15 = f32[2,128,128]{1,2,0:T(8,128)S(1)} custom-call(f32[2,128,128]{2,1,0:T(8,128)S(1)} %get-tuple-element.15), custom_call_target="InvertDiagBlocksLowerTriangular" | custom-call | tf_op jit(solution)/shard_map/triangular_solve | solution.py:161
  154.3 0.0 copy-start.3
  154.3 3.6 %fusion = f32[128,4096]{1,0:T(8,128)S(1)} fusion(f32[256,4096]{1,0:T(8,128)} %convert_add_fusion, f32[2,128,128]{1,2,0:T(8,128)S(1)} %custom-call.15), kind=kOutput, calls=%fused_computation.5 | convolution fusion | flops 805306368 | bytes 4259840 | tf_op jit(solution)/shard_map/triangular_solve | solution.py:161
  157.9 0.0 copy-done.3
  157.9 1.9 %convolution_subtract_fusion = f32[128,4096]{1,0:T(8,128)S(1)} fusion(f32[128,4096]{1,0:T(8,128)S(1)} %fusion, f32[256,4096]{1,0:T(8,128)S(1)} %copy-done.3, f32[256,256]{1,0:T(8,128)S(1)} %get-tuple-element.82), kind=kOutput, calls=%fused_computation.2 | convolution fusion | flops 805830656 | bytes 6356992 | tf_op jit(solution)/shard_map/triangular_solve | solution.py:161
  159.9 1.9 %fusion.6 = f32[128,4096]{1,0:T(8,128)S(1)} fusion(f32[128,4096]{1,0:T(8,128)S(1)} %convolution_subtract_fusion, f32[2,128,128]{1,2,0:T(8,128)S(1)} %custom-call.15), kind=kOutput, calls=%fused_computation.16 | convolution fusion | flops 805306368 | bytes 4259840 | tf_op jit(solution)/shard_map/triangular_solve | solution.py:161
  161.8 2.5 %pad_maximum_fusion = f32[256,4096]{1,0:T(8,128)} fusion(f32[128,4096]{1,0:T(8,128)S(1)} %fusion.6, f32[128,4096]{1,0:T(8,128)S(1)} %fusion), kind=kLoop, calls=%fused_computation.3 | loop fusion | flops 1048576 | bytes 8388608 | tf_op jit(solution)/shard_map/triangular_solve | solution.py:161
  (10 shorter events, 0.2 us)
Async XLA Ops:
  2.2 2.2 %copy-start = (f32[8,131072]{1,0:T(8,128)S(1)}, f32[8,131072]{1,0:T(8,128)}, u32[]{:S(2)}) copy-start(f32[8,131072]{1,0:T(8,128)} %anomaly.1) | copy-start | bytes 12582916
  4.3 1.0 copy-start.1
  5.4 1.0 copy-start.2
  154.3 3.7 %copy-start.3 = (f32[256,4096]{1,0:T(8,128)S(1)}, f32[256,4096]{1,0:T(8,128)}, u32[]{:S(2)}) copy-start(f32[256,4096]{1,0:T(8,128)} %convert_add_fusion) | copy-start | bytes 12582916

commit v2 on v1

--- a/solution.py
+++ b/solution.py
@@ -10,9 +10,9 @@
 CHUNKS = 4
 
 
-def gather_gram(n_band, n_dev, anomaly, area, mask, own_area, own_mask, hi_out, lo_out, gram_out,
-                land, hi, lo, hh, hl, part, piece_in, zsend, zin, agsend, gsum,
-                load_sem, a2a_send, a2a_recv, rs_send, rs_recv, z_send, z_recv, ag_send, ag_recv, out_sem):
+def gather_gram(n_band, n_dev, anomaly, area_hbm, mask_hbm, hi_out, lo_out, gram_out,
+                area, mask, land, hi, lo, hh, hl, part, piece_in, zsend, zin, agsend, gsum,
+                load_sem, area_sem, mask_sem, a2a_send, a2a_recv, rs_send, rs_recv, z_send, z_recv, ag_send, ag_recv, out_sem):
     z = lax.axis_index("band")
     me = lax.axis_index("dev")
     snaps, cells = land.shape
@@ -34,6 +34,10 @@
     own = pltpu.make_async_copy(anomaly.at[:, pl.ds(pl.multiple_of(me * cells, cells), cells)],
                                 land.at[pl.ds(pl.multiple_of(me * rows, rows), rows), :], load_sem)
     own.start()
+    get_area = pltpu.make_async_copy(area_hbm, area, area_sem)
+    get_mask = pltpu.make_async_copy(mask_hbm, mask, mask_sem)
+    get_area.start()
+    get_mask.start()
     pl.semaphore_wait(barrier, n_dev - 1 + n_band - 1)
 
     for c in range(CHUNKS):
@@ -47,8 +51,11 @@
             return _
         lax.fori_loop(1, n_dev, send, 0)
 
+    get_area.wait()
+    get_mask.wait()
     band_total = jnp.sum(area[...] * mask[...].astype(jnp.float32))
-    root = jnp.sqrt(own_area[...] * own_mask[...].astype(jnp.float32))
+    mine = pl.ds(pl.multiple_of(me * (cells // 128), 8), cells // 128)
+    root = jnp.sqrt(area[mine, :] * mask[mine, :].astype(jnp.float32))
     hh[...] = jnp.zeros_like(hh)
     hl[...] = jnp.zeros_like(hl)
     own.wait()
@@ -126,9 +133,6 @@
     snaps, cells = rows * n_dev, band_cells // n_dev
     area2 = area_weight.reshape(band_cells // 128, 128)
     mask2 = ocean_mask.reshape(band_cells // 128, 128)
-    at = lax.axis_index("dev") * (cells // 128)
-    own_area = lax.dynamic_slice_in_dim(area2, at, cells // 128, 0)
-    own_mask = lax.dynamic_slice_in_dim(mask2, at, cells // 128, 0)
     f32, bf16 = jnp.float32, jnp.bfloat16
     vmem = pl.BlockSpec(memory_space=pltpu.VMEM)
     hbm = pl.BlockSpec(memory_space=pl.ANY)
@@ -138,28 +142,163 @@
         name="gather_gram",
         out_shape=(jax.ShapeDtypeStruct((snaps, cells), bf16), jax.ShapeDtypeStruct((snaps, cells), bf16),
                    jax.ShapeDtypeStruct((snaps, snaps), f32)),
-        in_specs=[hbm, vmem, vmem, vmem, vmem],
+        in_specs=[hbm, hbm, hbm],
         out_specs=(hbm, hbm, vmem),
         scratch_shapes=[
+            pltpu.VMEM((band_cells // 128, 128), f32), pltpu.VMEM((band_cells // 128, 128), jnp.int32),
             pltpu.VMEM((snaps, cells), f32), pltpu.VMEM((snaps, cells), bf16), pltpu.VMEM((snaps, cells), bf16),
             pltpu.VMEM((snaps, snaps), f32), pltpu.VMEM((snaps, snaps), f32),
             pltpu.VMEM((n_dev, rows, snaps), f32), pltpu.VMEM((n_dev, rows, snaps), f32),
             pltpu.VMEM((rows, snaps + 128), f32), pltpu.VMEM((n_band, rows, snaps + 128), f32),
             pltpu.VMEM((rows, snaps), f32), pltpu.VMEM((n_dev, rows, snaps), f32),
-            dma, dma((CHUNKS,)), dma((CHUNKS,)), dma, dma, dma, dma, dma, dma, dma((2,)),
+            dma, dma, dma, dma((CHUNKS,)), dma((CHUNKS,)), dma, dma, dma, dma, dma, dma, dma((2,)),
         ],
         compiler_params=pltpu.CompilerParams(collective_id=0, has_side_effects=True, vmem_limit_bytes=40 * 1024 * 1024),
         cost_estimate=pl.CostEstimate(flops=4 * snaps * snaps * cells, bytes_accessed=8 * snaps * cells, transcendentals=0),
-    )(anomaly, area2, mask2, own_area, own_mask)
+    )(anomaly, area2, mask2)
+
+
+PANEL = 16
+TN = (((0,), (0,)), ((), ()))
+
+
+def split3(x):
+    a = x.astype(jnp.bfloat16)
+    rest = x - a.astype(jnp.float32)
+    b = rest.astype(jnp.bfloat16)
+    return a, b, (rest - b.astype(jnp.float32)).astype(jnp.bfloat16)
+
+
+def factor(work, upper, inverse):
+    n = work.shape[0]
+    row = lax.broadcasted_iota(jnp.int32, (8, 128), 0)
+    lane = lax.broadcasted_iota(jnp.int32, (8, 128), 1)
+    groups = PANEL // 8
+    tiles = n // 128
+    for k in range(n // PANEL):
+        base = k * PANEL
+        home, off = base // 128, base % 128
+        more = base + PANEL < n
+        inside = (lane >= off) & (lane < off + PANEL)
+        count = 2 * groups if more else groups
+        panel = [[work[base + 8 * s:base + 8 * s + 8, t * 128:(t + 1) * 128] for t in range(tiles)] for s in range(count)]
+        cols = [[jnp.broadcast_to(panel[s][home][:, off + c:off + c + 1], (8, 128)) for s in range(count)] for c in range(PANEL)]
+        diag = [panel[s][home] for s in range(groups)]
+        for s in range(count):
+            unit = jnp.where(lane == row + (off + 8 * s), 1.0, 0.0) if s < groups else 0.0
+            panel[s][home] = jnp.where(inside, unit, panel[s][home])
+        pivots = [None] * groups
+        for j in range(PANEL):
+            own, r = j // 8, j % 8
+            pivot = jnp.broadcast_to(cols[j][own][r:r + 1, :], (8, 128))
+            pivots[own] = pivot if r == 0 else jnp.where(row >= r, pivot, pivots[own])
+            inv = 1.0 / pivot
+            first = own if r < 7 else own + 1
+            mult = {}
+            for s in range(first, count):
+                m = jnp.where(row > r, cols[j][s], 0.0) if s == own else cols[j][s]
+                mult[s] = m * inv
+            for c in range(j + 1, PANEL):
+                line = jnp.broadcast_to(cols[c][own][r:r + 1, :], (8, 128))
+                for s in range(first, count):
+                    if s >= groups or 8 * s + 7 > j:
+                        cols[c][s] = cols[c][s] - mult[s] * line
+            for t in range(tiles):
+                line = jnp.broadcast_to(panel[own][t][r:r + 1, :], (8, 128))
+                for s in range(first, count):
+                    panel[s][t] = panel[s][t] - mult[s] * line
+            line = jnp.broadcast_to(diag[own][r:r + 1, :], (8, 128))
+            for s in range(first, groups):
+                diag[s] = diag[s] - mult[s] * line
+        for s in range(groups):
+            scale = lax.rsqrt(pivots[s])
+            at = pl.ds(base + 8 * s, 8)
+            for t in range(tiles):
+                val = panel[s][t] * scale
+                panel[s][t] = val
+                wide = pl.ds(t * 128, 128)
+                if t < home:
+                    inverse[at, wide] = val
+                    upper[at, wide] = jnp.zeros((8, 128), jnp.float32)
+                elif t > home:
+                    inverse[at, wide] = jnp.zeros((8, 128), jnp.float32)
+                    upper[at, wide] = val
+                else:
+                    inverse[at, wide] = jnp.where(lane <= row + (off + 8 * s), val, 0.0)
+                    u = jnp.where(inside, diag[s] * scale, val)
+                    upper[at, wide] = jnp.where(lane >= row + (off + 8 * s), u, 0.0)
+        if more:
+            for s in range(groups, count):
+                for t in range(tiles):
+                    work[base + 8 * s:base + 8 * s + 8, t * 128:(t + 1) * 128] = panel[s][t]
+        far = base + 2 * PANEL
+        if far < n:
+            lines = jnp.concatenate([jnp.concatenate(panel[s], axis=1) for s in range(groups)], axis=0)
+            a, b, c = split3(lines)
+            left = jnp.concatenate([a, a, b, a, b, c], axis=0)
+            right = jnp.concatenate([a, b, a, c, b, a], axis=0)
+            start = far // 128 * 128
+            delta = lax.dot_general(left[:, start:], right, TN, preferred_element_type=jnp.float32)
+            for i in range(far, n, 8):
+                for t in range(tiles):
+                    at, wide = slice(i, i + 8), slice(t * 128, (t + 1) * 128)
+                    old = work[at, wide]
+                    if t == home:
+                        old = jnp.where(inside, 0.0, old)
+                    work[at, wide] = old - delta[i - start:i - start + 8, wide]
+
+
+def solve(gram, hi_in, lo_in, upper, scores, work, inverse, hi, lo, out, in_sem, out_sem):
+    get_hi = pltpu.make_async_copy(hi_in, hi, in_sem.at[0])
+    get_lo = pltpu.make_async_copy(lo_in, lo, in_sem.at[1])
+    get_hi.start()
+    get_lo.start()
+    work[...] = gram[...]
+    factor(work, upper, inverse)
+    full = inverse[...]
+    top = full.astype(jnp.bfloat16)
+    rest = (full - top.astype(jnp.float32)).astype(jnp.bfloat16)
+    get_hi.wait()
+    get_lo.wait()
+    width = 512
+    puts = []
+    for c in range(hi.shape[1] // width):
+        at = pl.ds(c * width, width)
+        a, b = hi[:, at], lo[:, at]
+        out[:, at] = (jnp.dot(top, a, preferred_element_type=jnp.float32)
+                      + (jnp.dot(top, b, preferred_element_type=jnp.float32)
+                         + jnp.dot(rest, a, preferred_element_type=jnp.float32)))
+        put = pltpu.make_async_copy(out.at[:, at], scores.at[:, at], out_sem.at[c])
+        put.start()
+        puts.append(put)
+    for put in puts:
+        put.wait()
+
+
+def call_solve(gram, hi, lo):
+    snaps, cells = hi.shape
+    f32, bf16 = jnp.float32, jnp.bfloat16
+    vmem = pl.BlockSpec(memory_space=pltpu.VMEM)
+    hbm = pl.BlockSpec(memory_space=pl.ANY)
+    dma = pltpu.SemaphoreType.DMA
+    return pl.pallas_call(
+        solve,
+        name="solve",
+        out_shape=(jax.ShapeDtypeStruct((snaps, snaps), f32), jax.ShapeDtypeStruct((snaps, cells), f32)),
+        in_specs=[vmem, hbm, hbm],
+        out_specs=(vmem, hbm),
+        scratch_shapes=[pltpu.VMEM((snaps, snaps), f32), pltpu.VMEM((snaps, snaps), f32),
+                        pltpu.VMEM((snaps, cells), bf16), pltpu.VMEM((snaps, cells), bf16),
+                        pltpu.VMEM((snaps, cells), f32), dma((2,)), dma((cells // 512,))],
+        compiler_params=pltpu.CompilerParams(vmem_limit_bytes=40 * 1024 * 1024),
+        cost_estimate=pl.CostEstimate(flops=6 * snaps * snaps * cells, bytes_accessed=8 * snaps * cells, transcendentals=0),
+    )(gram, hi, lo)
 
 
 def solution(mesh):
     def on_device(anomaly, ocean_mask, area_weight):
         hi, lo, gram = call_gather_gram(mesh, anomaly, ocean_mask, area_weight)
-        lower = jnp.linalg.cholesky(gram)
-        scaled = hi.astype(jnp.float32) + lo.astype(jnp.float32)
-        scores = lax.linalg.triangular_solve(lower, scaled, left_side=True, lower=True)
-        return (lower.T, scores)
+        return call_solve(gram, hi, lo)
 
     return jax.shard_map(
         on_device,

time: 165 us -> 99 us (0.60)
  other arithmetic: 59.1 us -> 0 us
  Pallas kernels: 84.4 us -> 93.8 us
  matrix products: 7.99 us -> 0 us
  local copies, waits for them, and re-layouts: 10.7 us -> 4.26 us
    another operation x10 -> x0, other arithmetic: 56.4 us -> none  [the longest x6 34 us: on_device(): lower = jnp.linalg.cholesky(gram)]
    pallas_call x0 -> x1, Pallas kernels: none -> 9.44 us  [call_solve(): pl.pallas_call(solve, name='solve', out_shape=(jax.ShapeDtypeStruct((snap...]
    another operation x5 -> x0, matrix products: 7.99 us -> none  [the longest x3 7.52 us: on_device(): lax.linalg.triangular_solve(lower, scaled, left_side=True, lower=True)]
    another operation x9 -> x0, local copies, waits for them, and re-layouts: 4.04 us -> none
    add x1 -> x0, other arithmetic: 2.74 us -> none  [on_device(): scaled = hi.astype(jnp.float32) + lo.astype(jnp.float32)]
    unnamed x9 -> x6, local copies, waits for them, and re-layouts: 5.11 us -> 4.26 us
where the time goes in v2:
time: 99 us; the launch traced here: 98.7 us
  Pallas kernels  93.8 us (95%)
  local copies, waits for them, and re-layouts  4.26 us (4%)
    pallas_call x1, Pallas kernels, call_gather_gram(): pl.pallas_call(functools.partial(gather_gram, n_band, n_dev), name='gathe...  84.4 us
    pallas_call x1, Pallas kernels, call_solve(): pl.pallas_call(solve, name='solve', out_shape=(jax.ShapeDtypeStruct((snap...  9.44 us
    unnamed x6, local copies, waits for them, and re-layouts  4.26 us

profile of v2, /device:TPU:1, one launch (start us, length us, event | category | flops | bytes accessed | tf_op | source)
XLA Modules:
  0.0 98.7 jit_solution(15624903020761341748)
XLA Ops:
  0.6 0.0 copy-start
  0.6 2.2 %copy-done = f32[8,131072]{1,0:T(8,128)S(1)} copy-done((f32[8,131072]{1,0:T(8,128)S(1)}, f32[8,131072]{1,0:T(8,128)}, u32[]{:S(2)}) %copy-start) | copy-done | bytes 4194328
  2.8 0.0 copy-start.1
  2.8 1.0 %copy-done.1 = f32[131072]{0:T(1024)S(1)} copy-done((f32[131072]{0:T(1024)S(1)}, f32[131072]{0:T(1024)}, u32[]{:S(2)}) %copy-start.1) | copy-done | bytes 524312
  3.9 0.0 copy-start.2
  3.9 1.0 %copy-done.2 = s32[131072]{0:T(1024)S(1)} copy-done((s32[131072]{0:T(1024)S(1)}, s32[131072]{0:T(1024)}, u32[]{:S(2)}) %copy-start.2) | copy-done | bytes 524312
  4.9 84.4 %gather_gram.1 = (bf16[256,4096]{1,0:T(8,128)(2,1)S(1)}, bf16[256,4096]{1,0:T(8,128)(2,1)S(1)}, f32[256,256]{1,0:T(8,128)S(1)}) custom-call(f32[8,131072]{1,0:T(8,128)S(1)} %copy-done, f32[1024,128]{1,0:T(8,128)S(1)} %bitcast.2, s32[1024,128]{1,0:T(8,128)S(1)} %bitcast.3), custom_call_target="tpu_custom_call" | custom-call | flops 1073741824 | bytes 8388608 | tf_op jit(solution)/shard_map/gather_gram/pallas_call | solution.py:140
  89.3 9.4 %solve.1 = (f32[256,256]{1,0:T(8,128)}, f32[256,4096]{1,0:T(8,128)}) custom-call(f32[256,256]{1,0:T(8,128)S(1)} %get-tuple-element.5.gram, bf16[256,4096]{1,0:T(8,128)(2,1)S(1)} %get-tuple-element.6.hi_in, bf16[256,4096]{1,0:T(8,128)(2,1)S(1)} %get-tuple-element.7.lo_in), custom_call_target="tpu_custom_call" | custom-call | flops 1610612736 | bytes 8388608 | tf_op jit(solution)/shard_map/solve/pallas_call | solution.py:284
Async XLA Ops:
  0.6 2.2 %copy-start = (f32[8,131072]{1,0:T(8,128)S(1)}, f32[8,131072]{1,0:T(8,128)}, u32[]{:S(2)}) copy-start(f32[8,131072]{1,0:T(8,128)} %anomaly.1) | copy-start | bytes 12582916
  2.8 1.0 %copy-start.1 = (f32[131072]{0:T(1024)S(1)}, f32[131072]{0:T(1024)}, u32[]{:S(2)}) copy-start(f32[131072]{0:T(1024)} %param.5) | copy-start | bytes 1572868
  3.9 1.0 %copy-start.2 = (s32[131072]{0:T(1024)S(1)}, s32[131072]{0:T(1024)}, u32[]{:S(2)}) copy-start(s32[131072]{0:T(1024)} %param.4) | copy-start | bytes 1572868

commit v3 on v2

--- a/solution.py
+++ b/solution.py
@@ -7,30 +7,36 @@
 from jax.sharding import PartitionSpec as P
 
 MESH = pl.DeviceIdType.MESH
-CHUNKS = 4
+CHUNKS = 8
+SIDE = 4
+
+
+def ring(d, n):
+    return min(d, n - d)
+
+
+AROUND = sorted(((dx, dy, dc) for dx in range(SIDE) for dy in range(SIDE) for dc in range(2) if dx or dy or dc),
+                key=lambda o: -(ring(o[0], SIDE) + ring(o[1], SIDE)))
 
 
 def gather_gram(n_band, n_dev, anomaly, area_hbm, mask_hbm, hi_out, lo_out, gram_out,
-                area, mask, land, hi, lo, hh, hl, part, piece_in, zsend, zin, agsend, gsum,
+                area, mask, land, hi, lo, hh, part, piece_in, zsend, zin, agsend, gsum,
                 load_sem, area_sem, mask_sem, a2a_send, a2a_recv, rs_send, rs_recv, z_send, z_recv, ag_send, ag_recv, out_sem):
     z = lax.axis_index("band")
     me = lax.axis_index("dev")
+    x, y, core = me // (2 * SIDE), lax.rem(me, 2 * SIDE) // 2, lax.rem(me, 2)
+    peers = [lax.rem(x + dx, SIDE) * (2 * SIDE) + lax.rem(y + dy, SIDE) * 2 + lax.rem(core + dc, 2) for dx, dy, dc in AROUND]
+    levels = [lax.rem(z + dz, n_band) for dz in sorted(range(1, n_band), key=lambda d: -ring(d, n_band))]
     snaps, cells = land.shape
     rows = snaps // n_dev
     width = cells // CHUNKS
 
     barrier = pltpu.get_barrier_semaphore()
 
-    def greet(i, _):
-        pl.semaphore_signal(barrier, inc=1, device_id=(z, lax.rem(me + i, n_dev)), device_id_type=MESH)
-        return _
-
-    def greet_z(i, _):
-        pl.semaphore_signal(barrier, inc=1, device_id=(lax.rem(z + i, n_band), me), device_id_type=MESH)
-        return _
-
-    lax.fori_loop(1, n_dev, greet, 0)
-    lax.fori_loop(1, n_band, greet_z, 0)
+    for to in peers:
+        pl.semaphore_signal(barrier, inc=1, device_id=(z, to), device_id_type=MESH)
+    for to in levels:
+        pl.semaphore_signal(barrier, inc=1, device_id=(to, me), device_id_type=MESH)
     own = pltpu.make_async_copy(anomaly.at[:, pl.ds(pl.multiple_of(me * cells, cells), cells)],
                                 land.at[pl.ds(pl.multiple_of(me * rows, rows), rows), :], load_sem)
     own.start()
@@ -40,16 +46,16 @@
     get_mask.start()
     pl.semaphore_wait(barrier, n_dev - 1 + n_band - 1)
 
-    for c in range(CHUNKS):
-        def send(i, _, c=c):
-            to = lax.rem(me + i, n_dev)
+    def send_chunk(c, _):
+        column = pl.multiple_of(c * width, width)
+        for to in peers:
             pltpu.make_async_remote_copy(
-                src_ref=anomaly.at[:, pl.ds(pl.multiple_of(to * cells + c * width, width), width)],
-                dst_ref=land.at[pl.ds(pl.multiple_of(me * rows, rows), rows), pl.ds(c * width, width)],
+                src_ref=anomaly.at[:, pl.ds(pl.multiple_of(to * cells + column, width), width)],
+                dst_ref=land.at[pl.ds(pl.multiple_of(me * rows, rows), rows), pl.ds(column, width)],
                 send_sem=a2a_send.at[c], recv_sem=a2a_recv.at[c],
                 device_id=(z, to), device_id_type=MESH).start()
-            return _
-        lax.fori_loop(1, n_dev, send, 0)
+        return _
+    lax.fori_loop(0, CHUNKS, send_chunk, 0)
 
     get_area.wait()
     get_mask.wait()
@@ -57,7 +63,6 @@
     mine = pl.ds(pl.multiple_of(me * (cells // 128), 8), cells // 128)
     root = jnp.sqrt(area[mine, :] * mask[mine, :].astype(jnp.float32))
     hh[...] = jnp.zeros_like(hh)
-    hl[...] = jnp.zeros_like(hl)
     own.wait()
     nt = (((1,), (1,)), ((), ()))
     for c in range(CHUNKS):
@@ -71,22 +76,21 @@
             hi[:, at] = top
             lo[:, at] = (x - top.astype(jnp.float32)).astype(jnp.bfloat16)
         at = pl.ds(c * width, width)
-        hh[...] += lax.dot_general(hi[:, at], hi[:, at], nt, preferred_element_type=jnp.float32)
-        hl[...] += lax.dot_general(hi[:, at], lo[:, at], nt, preferred_element_type=jnp.float32)
+        a, b = hi[:, at], lo[:, at]
+        hh[...] += (lax.dot_general(a, a, nt, preferred_element_type=jnp.float32)
+                    + (lax.dot_general(a, b, nt, preferred_element_type=jnp.float32)
+                       + lax.dot_general(b, a, nt, preferred_element_type=jnp.float32)))
     put_hi = pltpu.make_async_copy(hi, hi_out, out_sem.at[0])
     put_lo = pltpu.make_async_copy(lo, lo_out, out_sem.at[1])
-    put_hi.start()
-    put_lo.start()
-    part[...] = (hh[...] + (hl[...] + hl[...].T)).reshape(n_dev, rows, snaps)
-
-    def send_piece(i, _):
-        to = lax.rem(me + i, n_dev)
+    part[...] = hh[...].reshape(n_dev, rows, snaps)
+
+    for to in peers:
         pltpu.make_async_remote_copy(
             src_ref=part.at[to], dst_ref=piece_in.at[me], send_sem=rs_send, recv_sem=rs_recv,
             device_id=(z, to), device_id_type=MESH).start()
-        return _
-    lax.fori_loop(1, n_dev, send_piece, 0)
     piece_in[me] = part[me]
+    put_hi.start()
+    put_lo.start()
     some = piece_in.at[pl.ds(0, n_dev - 1)]
     pltpu.make_async_copy(some, some, rs_recv).wait()
     piece = jnp.sum(piece_in[...], axis=0)
@@ -95,12 +99,10 @@
     zsend[:, snaps:] = jnp.full((rows, 128), band_total, jnp.float32)
     zin[z] = zsend[...]
 
-    def send_z(i, _):
+    for to in levels:
         pltpu.make_async_remote_copy(
             src_ref=zsend, dst_ref=zin.at[z], send_sem=z_send, recv_sem=z_recv,
-            device_id=(lax.rem(z + i, n_band), me), device_id_type=MESH).start()
-        return _
-    lax.fori_loop(1, n_band, send_z, 0)
+            device_id=(to, me), device_id_type=MESH).start()
     some_z = zin.at[pl.ds(0, n_band - 1)]
     pltpu.make_async_copy(some_z, some_z, z_recv).wait()
     summed = jnp.sum(zin[...], axis=0)
@@ -108,12 +110,10 @@
     agsend[...] = summed[:, :snaps] / jnp.concatenate([total, total], axis=1)
     gsum[me] = agsend[...]
 
-    def send_sum(i, _):
+    for to in peers:
         pltpu.make_async_remote_copy(
             src_ref=agsend, dst_ref=gsum.at[me], send_sem=ag_send, recv_sem=ag_recv,
-            device_id=(z, lax.rem(me + i, n_dev)), device_id_type=MESH).start()
-        return _
-    lax.fori_loop(1, n_dev, send_sum, 0)
+            device_id=(z, to), device_id_type=MESH).start()
     some_g = gsum.at[pl.ds(0, n_dev - 1)]
     pltpu.make_async_copy(some_g, some_g, ag_recv).wait()
     gram_out[...] = gsum[...].reshape(snaps, snaps)
@@ -135,7 +135,7 @@
     mask2 = ocean_mask.reshape(band_cells // 128, 128)
     f32, bf16 = jnp.float32, jnp.bfloat16
     vmem = pl.BlockSpec(memory_space=pltpu.VMEM)
-    hbm = pl.BlockSpec(memory_space=pl.ANY)
+    hbm = pl.BlockSpec(memory_space=pltpu.HBM)
     dma = pltpu.SemaphoreType.DMA
     return pl.pallas_call(
         functools.partial(gather_gram, n_band, n_dev),
@@ -147,7 +147,7 @@
         scratch_shapes=[
             pltpu.VMEM((band_cells // 128, 128), f32), pltpu.VMEM((band_cells // 128, 128), jnp.int32),
             pltpu.VMEM((snaps, cells), f32), pltpu.VMEM((snaps, cells), bf16), pltpu.VMEM((snaps, cells), bf16),
-            pltpu.VMEM((snaps, snaps), f32), pltpu.VMEM((snaps, snaps), f32),
+            pltpu.VMEM((snaps, snaps), f32),
             pltpu.VMEM((n_dev, rows, snaps), f32), pltpu.VMEM((n_dev, rows, snaps), f32),
             pltpu.VMEM((rows, snaps + 128), f32), pltpu.VMEM((n_band, rows, snaps + 128), f32),
             pltpu.VMEM((rows, snaps), f32), pltpu.VMEM((n_dev, rows, snaps), f32),
@@ -155,7 +155,7 @@
         ],
         compiler_params=pltpu.CompilerParams(collective_id=0, has_side_effects=True, vmem_limit_bytes=40 * 1024 * 1024),
         cost_estimate=pl.CostEstimate(flops=4 * snaps * snaps * cells, bytes_accessed=8 * snaps * cells, transcendentals=0),
-    )(anomaly, area2, mask2)
+    )(*[pltpu.with_memory_space_constraint(v, pltpu.HBM) for v in (anomaly, area2, mask2)])
 
 
 PANEL = 16
@@ -279,7 +279,7 @@
     snaps, cells = hi.shape
     f32, bf16 = jnp.float32, jnp.bfloat16
     vmem = pl.BlockSpec(memory_space=pltpu.VMEM)
-    hbm = pl.BlockSpec(memory_space=pl.ANY)
+    hbm = pl.BlockSpec(memory_space=pltpu.HBM)
     dma = pltpu.SemaphoreType.DMA
     return pl.pallas_call(
         solve,

time: 99 us -> 85.5 us (0.86)
  Pallas kernels: 93.8 us -> 84.8 us
  local copies, waits for them, and re-layouts: 4.26 us -> 0 us
    pallas_call x1, Pallas kernels: 84.4 us -> 75.4 us  [call_gather_gram(): pl.pallas_call(functools.partial(gather_gram, n_band, n_dev), name='gathe...]
    unnamed x6 -> x0, local copies, waits for them, and re-layouts: 4.26 us -> none
where the time goes in v3:
time: 85.5 us
  Pallas kernels  84.8 us (99%)
    pallas_call x1, Pallas kernels, call_gather_gram(): pl.pallas_call(functools.partial(gather_gram, n_band, n_dev), name='gathe...  75.4 us
    pallas_call x1, Pallas kernels, call_solve(): pl.pallas_call(solve, name='solve', out_shape=(jax.ShapeDtypeStruct((snap...  9.44 us

profile of v3, /device:TPU:1, one launch (start us, length us, event | category | flops | bytes accessed | tf_op | source)
XLA Modules:
  0.0 85.5 jit_solution(2852219249594351915)
XLA Ops:
  0.6 75.4 %gather_gram.1 = (bf16[256,4096]{1,0:T(8,128)(2,1)S(1)}, bf16[256,4096]{1,0:T(8,128)(2,1)S(1)}, f32[256,256]{1,0:T(8,128)S(1)}) custom-call(f32[8,131072]{1,0:T(8,128)} %anomaly.1, f32[1024,128]{1,0:T(8,128)} %bitcast.2, s32[1024,128]{1,0:T(8,128)} %bitcast.3), custom_call_target="tpu_custom_call" | custom-call | flops 1073741824 | bytes 8388608 | tf_op jit(solution)/shard_map/gather_gram/pallas_call | solution.py:140
  76.0 9.4 %solve.1 = (f32[256,256]{1,0:T(8,128)}, f32[256,4096]{1,0:T(8,128)}) custom-call(f32[256,256]{1,0:T(8,128)S(1)} %get-tuple-element.5.gram, bf16[256,4096]{1,0:T(8,128)(2,1)S(1)} %get-tuple-element.6.hi_in, bf16[256,4096]{1,0:T(8,128)(2,1)S(1)} %get-tuple-element.7.lo_in), custom_call_target="tpu_custom_call" | custom-call | flops 1610612736 | bytes 8388608 | tf_op jit(solution)/shard_map/solve/pallas_call | solution.py:284

commit v4 on v3

--- a/solution.py
+++ b/solution.py
@@ -19,9 +19,10 @@
                 key=lambda o: -(ring(o[0], SIDE) + ring(o[1], SIDE)))
 
 
-def gather_gram(n_band, n_dev, anomaly, area_hbm, mask_hbm, hi_out, lo_out, gram_out,
-                area, mask, land, hi, lo, hh, part, piece_in, zsend, zin, agsend, gsum,
-                load_sem, area_sem, mask_sem, a2a_send, a2a_recv, rs_send, rs_recv, z_send, z_recv, ag_send, ag_recv, out_sem):
+def gather_gram(n_band, n_dev, anomaly, area_hbm, mask_hbm, hi_out, lo_out, packed_out,
+                area, mask, land, hi, lo, gram, part, piece_in, extra_in, tsend, tin, zsend, zin, xsend, xin, agsend, gsum,
+                load_sem, area_sem, mask_sem, a2a_send, a2a_recv, rs_send, rs_recv, t_send, t_recv, z_send, z_recv,
+                ag_send, ag_recv, xr_send, xr_recv, xz_send, xz_recv, xa_send, xa_recv, out_sem):
     z = lax.axis_index("band")
     me = lax.axis_index("dev")
     x, y, core = me // (2 * SIDE), lax.rem(me, 2 * SIDE) // 2, lax.rem(me, 2)
@@ -46,6 +47,13 @@
     get_mask.start()
     pl.semaphore_wait(barrier, n_dev - 1 + n_band - 1)
 
+    def push(src, dst, send_sem, recv_sem, to):
+        pltpu.make_async_remote_copy(src_ref=src, dst_ref=dst, send_sem=send_sem, recv_sem=recv_sem,
+                                     device_id=to, device_id_type=MESH).start()
+
+    def drain(ref, sem):
+        pltpu.make_async_copy(ref, ref, sem).wait()
+
     def send_chunk(c, _):
         column = pl.multiple_of(c * width, width)
         for to in peers:
@@ -60,9 +68,13 @@
     get_area.wait()
     get_mask.wait()
     band_total = jnp.sum(area[...] * mask[...].astype(jnp.float32))
+    tsend[...] = jnp.full((rows, 128), band_total, jnp.float32)
+    tin[z] = tsend[...]
+    for to in levels:
+        push(tsend, tin.at[z], t_send, t_recv, (to, me))
     mine = pl.ds(pl.multiple_of(me * (cells // 128), 8), cells // 128)
     root = jnp.sqrt(area[mine, :] * mask[mine, :].astype(jnp.float32))
-    hh[...] = jnp.zeros_like(hh)
+    gram[...] = jnp.zeros_like(gram)
     own.wait()
     nt = (((1,), (1,)), ((), ()))
     for c in range(CHUNKS):
@@ -77,52 +89,91 @@
             lo[:, at] = (x - top.astype(jnp.float32)).astype(jnp.bfloat16)
         at = pl.ds(c * width, width)
         a, b = hi[:, at], lo[:, at]
-        hh[...] += (lax.dot_general(a, a, nt, preferred_element_type=jnp.float32)
+        gram[...] += (lax.dot_general(a, a, nt, preferred_element_type=jnp.float32)
                     + (lax.dot_general(a, b, nt, preferred_element_type=jnp.float32)
                        + lax.dot_general(b, a, nt, preferred_element_type=jnp.float32)))
+    row = lax.broadcasted_iota(jnp.int32, (8, 128), 0)
+    lane = lax.broadcasted_iota(jnp.int32, (8, 128), 1)
+    half = snaps // 2
+    tiles = half // 8
+    extra = jnp.zeros((8, 128), jnp.float32)
+    for p in range(tiles):
+        corner = gram[half + 8 * p:half + 8 * p + 8, half:]
+        part[p] = jnp.where(row + 8 * p <= lane, gram[8 * p:8 * p + 8, :half], corner)
+        part[tiles + p] = gram[8 * p:8 * p + 8, half:]
+        extra = jnp.where(row + 8 * p == lane, corner, extra)
+    part[2 * tiles] = extra
+    last = n_dev - 1
+
+    for to in peers:
+        push(part.at[to], piece_in.at[me], rs_send, rs_recv, (z, to))
+
+    @pl.when(me != last)
+    def _():
+        push(part.at[n_dev], extra_in.at[me], xr_send, xr_recv, (z, last))
+
+    piece_in[me] = part[me]
     put_hi = pltpu.make_async_copy(hi, hi_out, out_sem.at[0])
     put_lo = pltpu.make_async_copy(lo, lo_out, out_sem.at[1])
-    part[...] = hh[...].reshape(n_dev, rows, snaps)
-
-    for to in peers:
-        pltpu.make_async_remote_copy(
-            src_ref=part.at[to], dst_ref=piece_in.at[me], send_sem=rs_send, recv_sem=rs_recv,
-            device_id=(z, to), device_id_type=MESH).start()
-    piece_in[me] = part[me]
     put_hi.start()
     put_lo.start()
+    drain(tin.at[pl.ds(0, n_band - 1)], t_recv)
+    total = jnp.sum(tin[...], axis=0)
     some = piece_in.at[pl.ds(0, n_dev - 1)]
-    pltpu.make_async_copy(some, some, rs_recv).wait()
-    piece = jnp.sum(piece_in[...], axis=0)
-
-    zsend[:, :snaps] = piece
-    zsend[:, snaps:] = jnp.full((rows, 128), band_total, jnp.float32)
+    some_z = zin.at[pl.ds(0, n_band - 1)]
+    some_g = gsum.at[pl.ds(0, n_dev - 1)]
+    drain(some, rs_recv)
+    zsend[...] = jnp.sum(piece_in[...], axis=0)
+    for to in levels:
+        push(zsend, zin.at[z], z_send, z_recv, (to, me))
     zin[z] = zsend[...]
 
-    for to in levels:
-        pltpu.make_async_remote_copy(
-            src_ref=zsend, dst_ref=zin.at[z], send_sem=z_send, recv_sem=z_recv,
-            device_id=(to, me), device_id_type=MESH).start()
-    some_z = zin.at[pl.ds(0, n_band - 1)]
-    pltpu.make_async_copy(some_z, some_z, z_recv).wait()
-    summed = jnp.sum(zin[...], axis=0)
-    total = summed[:, snaps:]
-    agsend[...] = summed[:, :snaps] / jnp.concatenate([total, total], axis=1)
-    gsum[me] = agsend[...]
-
+    @pl.when(me == last)
+    def _():
+        extra_in[last] = part[n_dev]
+        drain(extra_in.at[pl.ds(0, n_dev - 1)], xr_recv)
+        xsend[...] = jnp.sum(extra_in[...], axis=0)
+        for to in levels:
+            push(xsend, xin.at[z], xz_send, xz_recv, (to, me))
+        xin[z] = xsend[...]
+
+    drain(some_z, z_recv)
+    agsend[0] = jnp.sum(zin[...], axis=0) / total
     for to in peers:
-        pltpu.make_async_remote_copy(
-            src_ref=agsend, dst_ref=gsum.at[me], send_sem=ag_send, recv_sem=ag_recv,
-            device_id=(z, to), device_id_type=MESH).start()
-    some_g = gsum.at[pl.ds(0, n_dev - 1)]
-    pltpu.make_async_copy(some_g, some_g, ag_recv).wait()
-    gram_out[...] = gsum[...].reshape(snaps, snaps)
-    pltpu.make_async_copy(some, some, rs_send).wait()
-    pltpu.make_async_copy(some_z, some_z, z_send).wait()
-    pltpu.make_async_copy(some_g, some_g, ag_send).wait()
+        push(agsend.at[0], gsum.at[me], ag_send, ag_recv, (z, to))
+    gsum[me] = agsend[0]
+
+    @pl.when(me == last)
+    def _():
+        drain(xin.at[pl.ds(0, n_band - 1)], xz_recv)
+        agsend[1] = jnp.sum(xin[...], axis=0) / total
+        for to in peers:
+            push(agsend.at[1], gsum.at[n_dev], xa_send, xa_recv, (z, to))
+        gsum[n_dev] = agsend[1]
+
+    drain(some_g, ag_recv)
+
+    @pl.when(me != last)
+    def _():
+        drain(gsum.at[n_dev], xa_recv)
+
+    packed_out[...] = gsum[...]
+
+    @pl.when(me != last)
+    def _():
+        drain(xsend, xr_send)
+
+    @pl.when(me == last)
+    def _():
+        drain(xin.at[pl.ds(0, n_band - 1)], xz_send)
+        drain(some_g, xa_send)
+
+    drain(some, rs_send)
+    drain(some_z, z_send)
+    drain(some_z, t_send)
+    drain(some_g, ag_send)
     for c in range(CHUNKS):
-        window = land.at[pl.ds(0, rows * (n_dev - 1)), pl.ds(c * width, width)]
-        pltpu.make_async_copy(window, window, a2a_send.at[c]).wait()
+        drain(land.at[pl.ds(0, rows * (n_dev - 1)), pl.ds(c * width, width)], a2a_send.at[c])
     put_hi.wait()
     put_lo.wait()
 
@@ -137,21 +188,24 @@
     vmem = pl.BlockSpec(memory_space=pltpu.VMEM)
     hbm = pl.BlockSpec(memory_space=pltpu.HBM)
     dma = pltpu.SemaphoreType.DMA
+
+    def tiles(count):
+        return pltpu.VMEM((count, rows, 128), f32)
+
     return pl.pallas_call(
         functools.partial(gather_gram, n_band, n_dev),
         name="gather_gram",
         out_shape=(jax.ShapeDtypeStruct((snaps, cells), bf16), jax.ShapeDtypeStruct((snaps, cells), bf16),
-                   jax.ShapeDtypeStruct((snaps, snaps), f32)),
+                   jax.ShapeDtypeStruct((n_dev + 1, rows, 128), f32)),
         in_specs=[hbm, hbm, hbm],
         out_specs=(hbm, hbm, vmem),
         scratch_shapes=[
             pltpu.VMEM((band_cells // 128, 128), f32), pltpu.VMEM((band_cells // 128, 128), jnp.int32),
             pltpu.VMEM((snaps, cells), f32), pltpu.VMEM((snaps, cells), bf16), pltpu.VMEM((snaps, cells), bf16),
-            pltpu.VMEM((snaps, snaps), f32),
-            pltpu.VMEM((n_dev, rows, snaps), f32), pltpu.VMEM((n_dev, rows, snaps), f32),
-            pltpu.VMEM((rows, snaps + 128), f32), pltpu.VMEM((n_band, rows, snaps + 128), f32),
-            pltpu.VMEM((rows, snaps), f32), pltpu.VMEM((n_dev, rows, snaps), f32),
-            dma, dma, dma, dma((CHUNKS,)), dma((CHUNKS,)), dma, dma, dma, dma, dma, dma, dma((2,)),
+            pltpu.VMEM((snaps, snaps), f32), tiles(n_dev + 1), tiles(n_dev), tiles(n_dev),
+            pltpu.VMEM((rows, 128), f32), tiles(n_band), pltpu.VMEM((rows, 128), f32), tiles(n_band),
+            pltpu.VMEM((rows, 128), f32), tiles(n_band), tiles(2), tiles(n_dev + 1),
+            dma, dma, dma, dma((CHUNKS,)), dma((CHUNKS,)), *[dma] * 14, dma((2,)),
         ],
         compiler_params=pltpu.CompilerParams(collective_id=0, has_side_effects=True, vmem_limit_bytes=40 * 1024 * 1024),
         cost_estimate=pl.CostEstimate(flops=4 * snaps * snaps * cells, bytes_accessed=8 * snaps * cells, transcendentals=0),
@@ -169,8 +223,10 @@
     return a, b, (rest - b.astype(jnp.float32)).astype(jnp.bfloat16)
 
 
-def factor(work, upper, inverse):
+def factor(work, upper, inverse, zero_ref, between):
     n = work.shape[0]
+    zero_ref[...] = jnp.zeros((8, 128), jnp.float32)
+    zero = zero_ref[...]
     row = lax.broadcasted_iota(jnp.int32, (8, 128), 0)
     lane = lax.broadcasted_iota(jnp.int32, (8, 128), 1)
     groups = PANEL // 8
@@ -182,7 +238,7 @@
         inside = (lane >= off) & (lane < off + PANEL)
         count = 2 * groups if more else groups
         panel = [[work[base + 8 * s:base + 8 * s + 8, t * 128:(t + 1) * 128] for t in range(tiles)] for s in range(count)]
-        cols = [[jnp.broadcast_to(panel[s][home][:, off + c:off + c + 1], (8, 128)) for s in range(count)] for c in range(PANEL)]
+        cols = [[jnp.broadcast_to(panel[s][home][:, off + c:off + c + 1], (8, 128)) + zero for s in range(count)] for c in range(PANEL)]
         diag = [panel[s][home] for s in range(groups)]
         for s in range(count):
             unit = jnp.where(lane == row + (off + 8 * s), 1.0, 0.0) if s < groups else 0.0
@@ -231,6 +287,7 @@
             for s in range(groups, count):
                 for t in range(tiles):
                     work[base + 8 * s:base + 8 * s + 8, t * 128:(t + 1) * 128] = panel[s][t]
+        between(k)
         far = base + 2 * PANEL
         if far < n:
             lines = jnp.concatenate([jnp.concatenate(panel[s], axis=1) for s in range(groups)], axis=0)
@@ -248,38 +305,75 @@
                     work[at, wide] = old - delta[i - start:i - start + 8, wide]
 
 
-def solve(gram, hi_in, lo_in, upper, scores, work, inverse, hi, lo, out, in_sem, out_sem):
+def unpack(packed, work):
+    half = work.shape[0] // 2
+    count = half // 8
+    row = lax.broadcasted_iota(jnp.int32, (half, half), 0)
+    lane = lax.broadcasted_iota(jnp.int32, (half, half), 1)
+    mixed = packed[:count].reshape(half, half)
+    cross = packed[count:2 * count].reshape(half, half)
+    diag = jnp.concatenate([packed[2 * count]] * count, axis=0)
+    turned = mixed.T
+    work[:half, :half] = jnp.where(row <= lane, mixed, turned)
+    work[:half, half:] = cross
+    work[half:, :half] = cross.T
+    work[half:, half:] = jnp.where(row > lane, mixed, jnp.where(row == lane, diag, turned))
+
+
+def solve(packed, hi_in, lo_in, upper, scores, work, inverse, zero, hi, lo, out, in_sem, out_sem):
     get_hi = pltpu.make_async_copy(hi_in, hi, in_sem.at[0])
     get_lo = pltpu.make_async_copy(lo_in, lo, in_sem.at[1])
     get_hi.start()
     get_lo.start()
-    work[...] = gram[...]
-    factor(work, upper, inverse)
-    full = inverse[...]
-    top = full.astype(jnp.bfloat16)
-    rest = (full - top.astype(jnp.float32)).astype(jnp.bfloat16)
-    get_hi.wait()
-    get_lo.wait()
+    unpack(packed, work)
+    n = work.shape[0]
+    half = n // 2
+    panels = n // PANEL
     width = 512
+    chunks = hi.shape[1] // width
+    held = []
     puts = []
-    for c in range(hi.shape[1] // width):
+
+    def split2(x):
+        a = x.astype(jnp.bfloat16)
+        return a, (x - a.astype(jnp.float32)).astype(jnp.bfloat16)
+
+    def put(rows, c):
         at = pl.ds(c * width, width)
-        a, b = hi[:, at], lo[:, at]
-        out[:, at] = (jnp.dot(top, a, preferred_element_type=jnp.float32)
-                      + (jnp.dot(top, b, preferred_element_type=jnp.float32)
-                         + jnp.dot(rest, a, preferred_element_type=jnp.float32)))
-        put = pltpu.make_async_copy(out.at[:, at], scores.at[:, at], out_sem.at[c])
-        put.start()
-        puts.append(put)
-    for put in puts:
-        put.wait()
-
-
-def call_solve(gram, hi, lo):
+        copy = pltpu.make_async_copy(out.at[rows, at], scores.at[rows, at], out_sem.at[len(puts)])
+        copy.start()
+        puts.append(copy)
+
+    def between(k):
+        if k == panels // 2 - 1:
+            get_hi.wait()
+            get_lo.wait()
+            a, b = split2(inverse[:half, :half])
+            held.append(jnp.concatenate([a, a, b], axis=1))
+        elif k >= panels // 2:
+            for c in range((k - panels // 2) * chunks * 2 // panels, (k + 1 - panels // 2) * chunks * 2 // panels):
+                at = pl.ds(c * width, width)
+                right = jnp.concatenate([hi[:half, at], lo[:half, at], hi[:half, at]], axis=0)
+                out[:half, at] = jnp.dot(held[0], right, preferred_element_type=jnp.float32)
+                put(pl.ds(0, half), c)
+
+    factor(work, upper, inverse, zero, between)
+    a, b = split2(inverse[half:, :])
+    both = jnp.concatenate([a, b], axis=0)
+    for c in range(chunks):
+        at = pl.ds(c * width, width)
+        ab = jnp.dot(both, hi[:, at], preferred_element_type=jnp.float32)
+        out[half:, at] = ab[:half] + (ab[half:] + jnp.dot(a, lo[:, at], preferred_element_type=jnp.float32))
+        put(pl.ds(half, half), c)
+    for copy in puts:
+        copy.wait()
+
+
+def call_solve(packed, hi, lo):
     snaps, cells = hi.shape
     f32, bf16 = jnp.float32, jnp.bfloat16
     vmem = pl.BlockSpec(memory_space=pltpu.VMEM)
-    hbm = pl.BlockSpec(memory_space=pltpu.HBM)
+    hbm = pl.BlockSpec(memory_space=pl.ANY)
     dma = pltpu.SemaphoreType.DMA
     return pl.pallas_call(
         solve,
@@ -287,18 +381,18 @@
         out_shape=(jax.ShapeDtypeStruct((snaps, snaps), f32), jax.ShapeDtypeStruct((snaps, cells), f32)),
         in_specs=[vmem, hbm, hbm],
         out_specs=(vmem, hbm),
-        scratch_shapes=[pltpu.VMEM((snaps, snaps), f32), pltpu.VMEM((snaps, snaps), f32),
+        scratch_shapes=[pltpu.VMEM((snaps, snaps), f32), pltpu.VMEM((snaps, snaps), f32), pltpu.VMEM((8, 128), f32),
                         pltpu.VMEM((snaps, cells), bf16), pltpu.VMEM((snaps, cells), bf16),
-                        pltpu.VMEM((snaps, cells), f32), dma((2,)), dma((cells // 512,))],
+                        pltpu.VMEM((snaps, cells), f32), dma((2,)), dma((2 * cells // 512,))],
         compiler_params=pltpu.CompilerParams(vmem_limit_bytes=40 * 1024 * 1024),
         cost_estimate=pl.CostEstimate(flops=6 * snaps * snaps * cells, bytes_accessed=8 * snaps * cells, transcendentals=0),
-    )(gram, hi, lo)
+    )(packed, hi, lo)
 
 
 def solution(mesh):
     def on_device(anomaly, ocean_mask, area_weight):
-        hi, lo, gram = call_gather_gram(mesh, anomaly, ocean_mask, area_weight)
-        return call_solve(gram, hi, lo)
+        hi, lo, packed = call_gather_gram(mesh, anomaly, ocean_mask, area_weight)
+        return call_solve(packed, hi, lo)
 
     return jax.shard_map(
         on_device,

time: 85.5 us -> 82.6 us (0.966)
  Pallas kernels: 84.8 us -> 81.8 us
    pallas_call x1, Pallas kernels: 75.4 us -> 73.7 us  [call_gather_gram(): pl.pallas_call(functools.partial(gather_gram, n_band, n_dev), name='gathe...]
    pallas_call x1, Pallas kernels: 9.44 us -> 8.12 us  [call_solve(): pl.pallas_call(solve, name='solve', out_shape=(jax.ShapeDtypeStruct((snap...]
where the time goes in v4:
time: 82.6 us; the launch traced here: 82.5 us
  Pallas kernels  81.8 us (99%)
    pallas_call x1, Pallas kernels, call_gather_gram(): pl.pallas_call(functools.partial(gather_gram, n_band, n_dev), name='gathe...  73.7 us
    pallas_call x1, Pallas kernels, call_solve(): pl.pallas_call(solve, name='solve', out_shape=(jax.ShapeDtypeStruct((snap...  8.12 us

profile of v4, /device:TPU:1, one launch (start us, length us, event | category | flops | bytes accessed | tf_op | source)
XLA Modules:
  0.0 82.5 jit_solution(2763631886576691951)
XLA Ops:
  0.6 73.7 %gather_gram.1 = (bf16[256,4096]{1,0:T(8,128)(2,1)S(1)}, bf16[256,4096]{1,0:T(8,128)(2,1)S(1)}, f32[33,8,128]{2,1,0:T(8,128)S(1)}) custom-call(f32[8,131072]{1,0:T(8,128)} %anomaly.1, f32[1024,128]{1,0:T(8,128)} %bitcast.2, s32[1024,128]{1,0:T(8,128)} %bitcast.3), custom_call_target="tpu_custom_call" | custom-call | flops 1073741824 | bytes 8388608 | tf_op jit(solution)/shard_map/gather_gram/pallas_call | solution.py:195
  74.4 8.1 %solve.1 = (f32[256,256]{1,0:T(8,128)}, f32[256,4096]{1,0:T(8,128)}) custom-call(f32[33,8,128]{2,1,0:T(8,128)S(1)} %get-tuple-element.5.packed, bf16[256,4096]{1,0:T(8,128)(2,1)S(1)} %get-tuple-element.6.hi_in, bf16[256,4096]{1,0:T(8,128)(2,1)S(1)} %get-tuple-element.7.lo_in), custom_call_target="tpu_custom_call" | custom-call | flops 1610612736 | bytes 8388608 | tf_op jit(solution)/shard_map/solve/pallas_call | solution.py:378

commit v5 on v4

--- a/solution.py
+++ b/solution.py
@@ -20,9 +20,9 @@
 
 
 def gather_gram(n_band, n_dev, anomaly, area_hbm, mask_hbm, hi_out, lo_out, packed_out,
-                area, mask, land, hi, lo, gram, part, piece_in, extra_in, tsend, tin, zsend, zin, xsend, xin, agsend, gsum,
+                area, mask, land, hi, lo, gram, part, piece_in, extra_in, tsend, tin, zsend, zin, xsend, xin, agsend,
                 load_sem, area_sem, mask_sem, a2a_send, a2a_recv, rs_send, rs_recv, t_send, t_recv, z_send, z_recv,
-                ag_send, ag_recv, xr_send, xr_recv, xz_send, xz_recv, xa_send, xa_recv, out_sem):
+                ag_send, ag_recv, xr_send, xr_recv, xz_send, xz_recv, xa_send, xa_recv, keep_sem, keep_extra_sem, out_sem):
     z = lax.axis_index("band")
     me = lax.axis_index("dev")
     x, y, core = me // (2 * SIDE), lax.rem(me, 2 * SIDE) // 2, lax.rem(me, 2)
@@ -77,6 +77,7 @@
     gram[...] = jnp.zeros_like(gram)
     own.wait()
     nt = (((1,), (1,)), ((), ()))
+    done = []
     for c in range(CHUNKS):
         window = land.at[pl.ds(0, rows * (n_dev - 1)), pl.ds(c * width, width)]
         pltpu.make_async_copy(window, window, a2a_recv.at[c]).wait()
@@ -88,6 +89,11 @@
             hi[:, at] = top
             lo[:, at] = (x - top.astype(jnp.float32)).astype(jnp.bfloat16)
         at = pl.ds(c * width, width)
+        puts = [pltpu.make_async_copy(hi.at[:, at], hi_out.at[:, at], out_sem.at[2 * c]),
+                pltpu.make_async_copy(lo.at[:, at], lo_out.at[:, at], out_sem.at[2 * c + 1])]
+        for put in puts:
+            put.start()
+        done.extend(puts)
         a, b = hi[:, at], lo[:, at]
         gram[...] += (lax.dot_general(a, a, nt, preferred_element_type=jnp.float32)
                     + (lax.dot_general(a, b, nt, preferred_element_type=jnp.float32)
@@ -113,15 +119,11 @@
         push(part.at[n_dev], extra_in.at[me], xr_send, xr_recv, (z, last))
 
     piece_in[me] = part[me]
-    put_hi = pltpu.make_async_copy(hi, hi_out, out_sem.at[0])
-    put_lo = pltpu.make_async_copy(lo, lo_out, out_sem.at[1])
-    put_hi.start()
-    put_lo.start()
     drain(tin.at[pl.ds(0, n_band - 1)], t_recv)
     total = jnp.sum(tin[...], axis=0)
     some = piece_in.at[pl.ds(0, n_dev - 1)]
     some_z = zin.at[pl.ds(0, n_band - 1)]
-    some_g = gsum.at[pl.ds(0, n_dev - 1)]
+    some_g = packed_out.at[pl.ds(0, n_dev - 1)]
     drain(some, rs_recv)
     zsend[...] = jnp.sum(piece_in[...], axis=0)
     for to in levels:
@@ -140,24 +142,27 @@
     drain(some_z, z_recv)
     agsend[0] = jnp.sum(zin[...], axis=0) / total
     for to in peers:
-        push(agsend.at[0], gsum.at[me], ag_send, ag_recv, (z, to))
-    gsum[me] = agsend[0]
+        push(agsend.at[0], packed_out.at[me], ag_send, ag_recv, (z, to))
+    keep = pltpu.make_async_copy(agsend.at[0], packed_out.at[me], keep_sem)
+    keep.start()
 
     @pl.when(me == last)
     def _():
         drain(xin.at[pl.ds(0, n_band - 1)], xz_recv)
         agsend[1] = jnp.sum(xin[...], axis=0) / total
         for to in peers:
-            push(agsend.at[1], gsum.at[n_dev], xa_send, xa_recv, (z, to))
-        gsum[n_dev] = agsend[1]
+            push(agsend.at[1], packed_out.at[n_dev], xa_send, xa_recv, (z, to))
+        keep_extra = pltpu.make_async_copy(agsend.at[1], packed_out.at[n_dev], keep_extra_sem)
+        keep_extra.start()
+        keep_extra.wait()
 
     drain(some_g, ag_recv)
 
     @pl.when(me != last)
     def _():
-        drain(gsum.at[n_dev], xa_recv)
-
-    packed_out[...] = gsum[...]
+        drain(packed_out.at[n_dev], xa_recv)
+
+    keep.wait()
 
     @pl.when(me != last)
     def _():
@@ -174,8 +179,8 @@
     drain(some_g, ag_send)
     for c in range(CHUNKS):
         drain(land.at[pl.ds(0, rows * (n_dev - 1)), pl.ds(c * width, width)], a2a_send.at[c])
-    put_hi.wait()
-    put_lo.wait()
+    for put in done:
+        put.wait()
 
 
 def call_gather_gram(mesh, anomaly, ocean_mask, area_weight):
@@ -198,14 +203,14 @@
         out_shape=(jax.ShapeDtypeStruct((snaps, cells), bf16), jax.ShapeDtypeStruct((snaps, cells), bf16),
                    jax.ShapeDtypeStruct((n_dev + 1, rows, 128), f32)),
         in_specs=[hbm, hbm, hbm],
-        out_specs=(hbm, hbm, vmem),
+        out_specs=(hbm, hbm, hbm),
         scratch_shapes=[
             pltpu.VMEM((band_cells // 128, 128), f32), pltpu.VMEM((band_cells // 128, 128), jnp.int32),
             pltpu.VMEM((snaps, cells), f32), pltpu.VMEM((snaps, cells), bf16), pltpu.VMEM((snaps, cells), bf16),
             pltpu.VMEM((snaps, snaps), f32), tiles(n_dev + 1), tiles(n_dev), tiles(n_dev),
             pltpu.VMEM((rows, 128), f32), tiles(n_band), pltpu.VMEM((rows, 128), f32), tiles(n_band),
-            pltpu.VMEM((rows, 128), f32), tiles(n_band), tiles(2), tiles(n_dev + 1),
-            dma, dma, dma, dma((CHUNKS,)), dma((CHUNKS,)), *[dma] * 14, dma((2,)),
+            pltpu.VMEM((rows, 128), f32), tiles(n_band), tiles(2),
+            dma, dma, dma, dma((CHUNKS,)), dma((CHUNKS,)), *[dma] * 16, dma((2 * CHUNKS,)),
         ],
         compiler_params=pltpu.CompilerParams(collective_id=0, has_side_effects=True, vmem_limit_bytes=40 * 1024 * 1024),
         cost_estimate=pl.CostEstimate(flops=4 * snaps * snaps * cells, bytes_accessed=8 * snaps * cells, transcendentals=0),
@@ -238,7 +243,8 @@
         inside = (lane >= off) & (lane < off + PANEL)
         count = 2 * groups if more else groups
         panel = [[work[base + 8 * s:base + 8 * s + 8, t * 128:(t + 1) * 128] for t in range(tiles)] for s in range(count)]
-        cols = [[jnp.broadcast_to(panel[s][home][:, off + c:off + c + 1], (8, 128)) + zero for s in range(count)] for c in range(PANEL)]
+        cols = [[jnp.broadcast_to(panel[s][home][:, off + c:off + c + 1], (8, 128)) for s in range(count)] for c in range(PANEL)]
+        cols[0] = [v + zero for v in cols[0][:groups]] + cols[0][groups:]
         diag = [panel[s][home] for s in range(groups)]
         for s in range(count):
             unit = jnp.where(lane == row + (off + 8 * s), 1.0, 0.0) if s < groups else 0.0
@@ -255,10 +261,9 @@
                 m = jnp.where(row > r, cols[j][s], 0.0) if s == own else cols[j][s]
                 mult[s] = m * inv
             for c in range(j + 1, PANEL):
-                line = jnp.broadcast_to(cols[c][own][r:r + 1, :], (8, 128))
-                for s in range(first, count):
-                    if s >= groups or 8 * s + 7 > j:
-                        cols[c][s] = cols[c][s] - mult[s] * line
+                line = jnp.broadcast_to(cols[j][c // 8][c % 8:c % 8 + 1, :], (8, 128))
+                for s in range(max(first, c // 8), count):
+                    cols[c][s] = cols[c][s] - mult[s] * line
             for t in range(tiles):
                 line = jnp.broadcast_to(panel[own][t][r:r + 1, :], (8, 128))
                 for s in range(first, count):
@@ -320,7 +325,7 @@
     work[half:, half:] = jnp.where(row > lane, mixed, jnp.where(row == lane, diag, turned))
 
 
-def solve(packed, hi_in, lo_in, upper, scores, work, inverse, zero, hi, lo, out, in_sem, out_sem):
+def solve(packed, hi_in, lo_in, factor_out, scores, work, upper, inverse, zero, hi, lo, out, in_sem, factor_sem, out_sem):
     get_hi = pltpu.make_async_copy(hi_in, hi, in_sem.at[0])
     get_lo = pltpu.make_async_copy(lo_in, lo, in_sem.at[1])
     get_hi.start()
@@ -358,6 +363,8 @@
                 put(pl.ds(0, half), c)
 
     factor(work, upper, inverse, zero, between)
+    put_factor = pltpu.make_async_copy(upper, factor_out, factor_sem)
+    put_factor.start()
     a, b = split2(inverse[half:, :])
     both = jnp.concatenate([a, b], axis=0)
     for c in range(chunks):
@@ -367,6 +374,7 @@
         put(pl.ds(half, half), c)
     for copy in puts:
         copy.wait()
+    put_factor.wait()
 
 
 def call_solve(packed, hi, lo):
@@ -380,10 +388,11 @@
         name="solve",
         out_shape=(jax.ShapeDtypeStruct((snaps, snaps), f32), jax.ShapeDtypeStruct((snaps, cells), f32)),
         in_specs=[vmem, hbm, hbm],
-        out_specs=(vmem, hbm),
-        scratch_shapes=[pltpu.VMEM((snaps, snaps), f32), pltpu.VMEM((snaps, snaps), f32), pltpu.VMEM((8, 128), f32),
+        out_specs=(hbm, hbm),
+        scratch_shapes=[pltpu.VMEM((snaps, snaps), f32), pltpu.VMEM((snaps, snaps), f32), pltpu.VMEM((snaps, snaps), f32),
+                        pltpu.VMEM((8, 128), f32),
                         pltpu.VMEM((snaps, cells), bf16), pltpu.VMEM((snaps, cells), bf16),
-                        pltpu.VMEM((snaps, cells), f32), dma((2,)), dma((2 * cells // 512,))],
+                        pltpu.VMEM((snaps, cells), f32), dma((2,)), dma, dma((2 * cells // 512,))],
         compiler_params=pltpu.CompilerParams(vmem_limit_bytes=40 * 1024 * 1024),
         cost_estimate=pl.CostEstimate(flops=6 * snaps * snaps * cells, bytes_accessed=8 * snaps * cells, transcendentals=0),
     )(packed, hi, lo)

time: 82.6 us -> 82.1 us (level)
    pallas_call x1, Pallas kernels: 8.12 us -> 7.27 us  [call_solve(): pl.pallas_call(solve, name='solve', out_shape=(jax.ShapeDtypeStruct((snap...]
where the time goes in v5:
time: 82.1 us; the launch traced here: 82 us
  Pallas kernels  81.4 us (99%)
    pallas_call x1, Pallas kernels, call_gather_gram(): pl.pallas_call(functools.partial(gather_gram, n_band, n_dev), name='gathe...  74.1 us
    pallas_call x1, Pallas kernels, call_solve(): pl.pallas_call(solve, name='solve', out_shape=(jax.ShapeDtypeStruct((snap...  7.27 us

profile of v5, /device:TPU:1, one launch (start us, length us, event | category | flops | bytes accessed | tf_op | source)
XLA Modules:
  0.0 82.0 jit_solution(3649093869022656689)
XLA Ops:
  0.6 74.1 %gather_gram.1 = (bf16[256,4096]{1,0:T(8,128)(2,1)S(1)}, bf16[256,4096]{1,0:T(8,128)(2,1)S(1)}, f32[33,8,128]{2,1,0:T(8,128)S(1)}) custom-call(f32[8,131072]{1,0:T(8,128)} %anomaly.1, f32[1024,128]{1,0:T(8,128)} %bitcast.2, s32[1024,128]{1,0:T(8,128)} %bitcast.3), custom_call_target="tpu_custom_call" | custom-call | flops 1073741824 | bytes 8388608 | tf_op jit(solution)/shard_map/gather_gram/pallas_call | solution.py:200
  74.7 7.3 %solve.1 = (f32[256,256]{1,0:T(8,128)}, f32[256,4096]{1,0:T(8,128)}) custom-call(f32[33,8,128]{2,1,0:T(8,128)S(1)} %get-tuple-element.5.packed, bf16[256,4096]{1,0:T(8,128)(2,1)S(1)} %get-tuple-element.6.hi_in, bf16[256,4096]{1,0:T(8,128)(2,1)S(1)} %get-tuple-element.7.lo_in), custom_call_target="tpu_custom_call" | custom-call | flops 1610612736 | bytes 8388608 | tf_op jit(solution)/shard_map/solve/pallas_call | solution.py:386

commit v6 on v5

--- a/solution.py
+++ b/solution.py
@@ -19,10 +19,10 @@
                 key=lambda o: -(ring(o[0], SIDE) + ring(o[1], SIDE)))
 
 
-def gather_gram(n_band, n_dev, anomaly, area_hbm, mask_hbm, hi_out, lo_out, packed_out,
-                area, mask, land, hi, lo, gram, part, piece_in, extra_in, tsend, tin, zsend, zin, xsend, xin, agsend,
+def gather_gram(n_band, n_dev, anomaly, area_hbm, mask_hbm, hi, lo, packed_out,
+                area, mask, land, gram, part, piece_in, extra_in, tsend, tin, zsend, zin, xsend, xin, agsend,
                 load_sem, area_sem, mask_sem, a2a_send, a2a_recv, rs_send, rs_recv, t_send, t_recv, z_send, z_recv,
-                ag_send, ag_recv, xr_send, xr_recv, xz_send, xz_recv, xa_send, xa_recv, keep_sem, keep_extra_sem, out_sem):
+                ag_send, ag_recv, xr_send, xr_recv, xz_send, xz_recv, xa_send, xa_recv, keep_sem, keep_extra_sem):
     z = lax.axis_index("band")
     me = lax.axis_index("dev")
     x, y, core = me // (2 * SIDE), lax.rem(me, 2 * SIDE) // 2, lax.rem(me, 2)
@@ -77,7 +77,6 @@
     gram[...] = jnp.zeros_like(gram)
     own.wait()
     nt = (((1,), (1,)), ((), ()))
-    done = []
     for c in range(CHUNKS):
         window = land.at[pl.ds(0, rows * (n_dev - 1)), pl.ds(c * width, width)]
         pltpu.make_async_copy(window, window, a2a_recv.at[c]).wait()
@@ -89,11 +88,6 @@
             hi[:, at] = top
             lo[:, at] = (x - top.astype(jnp.float32)).astype(jnp.bfloat16)
         at = pl.ds(c * width, width)
-        puts = [pltpu.make_async_copy(hi.at[:, at], hi_out.at[:, at], out_sem.at[2 * c]),
-                pltpu.make_async_copy(lo.at[:, at], lo_out.at[:, at], out_sem.at[2 * c + 1])]
-        for put in puts:
-            put.start()
-        done.extend(puts)
         a, b = hi[:, at], lo[:, at]
         gram[...] += (lax.dot_general(a, a, nt, preferred_element_type=jnp.float32)
                     + (lax.dot_general(a, b, nt, preferred_element_type=jnp.float32)
@@ -179,8 +173,6 @@
     drain(some_g, ag_send)
     for c in range(CHUNKS):
         drain(land.at[pl.ds(0, rows * (n_dev - 1)), pl.ds(c * width, width)], a2a_send.at[c])
-    for put in done:
-        put.wait()
 
 
 def call_gather_gram(mesh, anomaly, ocean_mask, area_weight):
@@ -203,14 +195,14 @@
         out_shape=(jax.ShapeDtypeStruct((snaps, cells), bf16), jax.ShapeDtypeStruct((snaps, cells), bf16),
                    jax.ShapeDtypeStruct((n_dev + 1, rows, 128), f32)),
         in_specs=[hbm, hbm, hbm],
-        out_specs=(hbm, hbm, hbm),
+        out_specs=(vmem, vmem, hbm),
         scratch_shapes=[
             pltpu.VMEM((band_cells // 128, 128), f32), pltpu.VMEM((band_cells // 128, 128), jnp.int32),
-            pltpu.VMEM((snaps, cells), f32), pltpu.VMEM((snaps, cells), bf16), pltpu.VMEM((snaps, cells), bf16),
+            pltpu.VMEM((snaps, cells), f32),
             pltpu.VMEM((snaps, snaps), f32), tiles(n_dev + 1), tiles(n_dev), tiles(n_dev),
             pltpu.VMEM((rows, 128), f32), tiles(n_band), pltpu.VMEM((rows, 128), f32), tiles(n_band),
             pltpu.VMEM((rows, 128), f32), tiles(n_band), tiles(2),
-            dma, dma, dma, dma((CHUNKS,)), dma((CHUNKS,)), *[dma] * 16, dma((2 * CHUNKS,)),
+            dma, dma, dma, dma((CHUNKS,)), dma((CHUNKS,)), *[dma] * 16,
         ],
         compiler_params=pltpu.CompilerParams(collective_id=0, has_side_effects=True, vmem_limit_bytes=40 * 1024 * 1024),
         cost_estimate=pl.CostEstimate(flops=4 * snaps * snaps * cells, bytes_accessed=8 * snaps * cells, transcendentals=0),
@@ -325,11 +317,7 @@
     work[half:, half:] = jnp.where(row > lane, mixed, jnp.where(row == lane, diag, turned))
 
 
-def solve(packed, hi_in, lo_in, factor_out, scores, work, upper, inverse, zero, hi, lo, out, in_sem, factor_sem, out_sem):
-    get_hi = pltpu.make_async_copy(hi_in, hi, in_sem.at[0])
-    get_lo = pltpu.make_async_copy(lo_in, lo, in_sem.at[1])
-    get_hi.start()
-    get_lo.start()
+def solve(packed, hi, lo, factor_out, scores, work, upper, inverse, zero, out, factor_sem, out_sem):
     unpack(packed, work)
     n = work.shape[0]
     half = n // 2
@@ -351,8 +339,6 @@
 
     def between(k):
         if k == panels // 2 - 1:
-            get_hi.wait()
-            get_lo.wait()
             a, b = split2(inverse[:half, :half])
             held.append(jnp.concatenate([a, a, b], axis=1))
         elif k >= panels // 2:
@@ -387,12 +373,11 @@
         solve,
         name="solve",
         out_shape=(jax.ShapeDtypeStruct((snaps, snaps), f32), jax.ShapeDtypeStruct((snaps, cells), f32)),
-        in_specs=[vmem, hbm, hbm],
+        in_specs=[vmem, vmem, vmem],
         out_specs=(hbm, hbm),
         scratch_shapes=[pltpu.VMEM((snaps, snaps), f32), pltpu.VMEM((snaps, snaps), f32), pltpu.VMEM((snaps, snaps), f32),
                         pltpu.VMEM((8, 128), f32),
-                        pltpu.VMEM((snaps, cells), bf16), pltpu.VMEM((snaps, cells), bf16),
-                        pltpu.VMEM((snaps, cells), f32), dma((2,)), dma, dma((2 * cells // 512,))],
+                        pltpu.VMEM((snaps, cells), f32), dma, dma((2 * cells // 512,))],
         compiler_params=pltpu.CompilerParams(vmem_limit_bytes=40 * 1024 * 1024),
         cost_estimate=pl.CostEstimate(flops=6 * snaps * snaps * cells, bytes_accessed=8 * snaps * cells, transcendentals=0),
     )(packed, hi, lo)

time: 82.1 us -> 81.4 us (level)
  no operation moved by 1% of the time
where the time goes in v6:
time: 81.4 us; the launch traced here: 81.3 us
  Pallas kernels  80.7 us (99%)
    pallas_call x1, Pallas kernels, call_gather_gram(): pl.pallas_call(functools.partial(gather_gram, n_band, n_dev), name='gathe...  73.7 us
    pallas_call x1, Pallas kernels, call_solve(): pl.pallas_call(solve, name='solve', out_shape=(jax.ShapeDtypeStruct((snap...  6.97 us

profile of v6, /device:TPU:1, one launch (start us, length us, event | category | flops | bytes accessed | tf_op | source)
XLA Modules:
  0.0 81.3 jit_solution(16408563585620172880)
XLA Ops:
  0.6 73.7 %gather_gram.1 = (bf16[256,4096]{1,0:T(8,128)(2,1)S(1)}, bf16[256,4096]{1,0:T(8,128)(2,1)S(1)}, f32[33,8,128]{2,1,0:T(8,128)S(1)}) custom-call(f32[8,131072]{1,0:T(8,128)} %anomaly.1, f32[1024,128]{1,0:T(8,128)} %bitcast.2, s32[1024,128]{1,0:T(8,128)} %bitcast.3), custom_call_target="tpu_custom_call" | custom-call | flops 1073741824 | bytes 8388608 | tf_op jit(solution)/shard_map/gather_gram/pallas_call | solution.py:192
  74.3 7.0 %solve.1 = (f32[256,256]{1,0:T(8,128)}, f32[256,4096]{1,0:T(8,128)}) custom-call(f32[33,8,128]{2,1,0:T(8,128)S(1)} %get-tuple-element.5.packed, bf16[256,4096]{1,0:T(8,128)(2,1)S(1)} %get-tuple-element.6.hi, bf16[256,4096]{1,0:T(8,128)(2,1)S(1)} %get-tuple-element.7.lo), custom_call_target="tpu_custom_call" | custom-call | flops 1610612736 | bytes 8388608 | tf_op jit(solution)/shard_map/solve/pallas_call | solution.py:372
